TPU v7x, 32 devices: a whole 2x2x4 slice. The times are simulated.
32 devices in a mesh: groups: 2 (over x), wide: 16 (over z, y, core).
Axes of the slice: x: 2, y: 2, z: 4, core: 2. Of those that a mesh axis runs over, the one named last changes fastest.
Arguments:
- video: bfloat16 [64, 1024, 1152], P(('groups', 'wide')), parts along dimension 0, may hold values from -40 to 40
- modulation: float32 [12, 1152], P('groups'), parts along dimension 0, may hold values from -3 to 3
- spatial_input: bfloat16 [1152, 3456], replicated, may hold values from -1 to 1
- spatial_output: bfloat16 [1152, 1152], replicated, may hold values from -0.1875 to 0.1875
- temporal_input: bfloat16 [1152, 3456], replicated, may hold values from -1 to 1
- temporal_output: bfloat16 [1152, 1152], replicated, may hold values from -0.1875 to 0.1875
Outputs:
- refined: bfloat16 [64, 1024, 1152], P(('groups', 'wide')), parts along dimension 0
There are 2 independent parts, one for each index of `groups`. A program takes and returns all parts, laid end to end along the dimension named above; an argument that names none is the same for every part. Nothing has to cross between parts.
All inputs are finite; a program needn't handle non-finite values.
Results may differ from a plain program's by a relative error of at most 0.0052.
Values may be sent and summed in bfloat16 or wider, within the bound.
No kernel may reach another device: no remote copies, remote signals or barrier semaphores. Data moves between devices by JAX's collectives and lax.ppermute only.
A program may use at most 320 MiB of HBM per device.

v0:
```python
import math
import jax
import jax.numpy as jnp
from jax import lax
from jax.sharding import PartitionSpec as P

HEADS = 16
HEAD_DIM = 72
epsilon = 1e-06


def normalize(stream, offset_row, stretch):
    values = stream.astype(jnp.float32)
    average = jnp.mean(values, axis=-1, keepdims=True)
    centered = values - average
    spread = jnp.mean(centered * centered, axis=-1, keepdims=True)
    return (centered * lax.rsqrt(spread + epsilon) * (1.0 + stretch) + offset_row).astype(
        jnp.bfloat16
    )


def attend_space(video, modulation, spatial_input, spatial_output):
    count_local, length, features = video.shape
    score_scale = 1.0 / math.sqrt(HEAD_DIM)
    normed = normalize(video, modulation[0], modulation[1])
    triples = jnp.dot(
        normed.reshape(count_local * length, features),
        spatial_input,
        preferred_element_type=jnp.float32,
    )
    triples = triples.astype(jnp.bfloat16).reshape(count_local, length, 3, HEADS, HEAD_DIM)
    scores = (
        jnp.einsum(
            "fqhd,fkhd->fhqk",
            triples[:, :, 0],
            triples[:, :, 1],
            preferred_element_type=jnp.float32,
        )
        * score_scale
    )
    weights = jax.nn.softmax(scores, axis=-1).astype(jnp.bfloat16)
    attended = jnp.einsum(
        "fhqk,fkhd->fqhd", weights, triples[:, :, 2], preferred_element_type=jnp.float32
    ).astype(jnp.bfloat16)
    branch = jnp.dot(
        attended.reshape(count_local * length, features),
        spatial_output,
        preferred_element_type=jnp.float32,
    )
    return (
        video.astype(jnp.float32) + modulation[2] * branch.reshape(count_local, length, features)
    ).astype(jnp.bfloat16)


def attend_time(triples):
    frames, sites, triple_width = triples.shape
    score_scale = 1.0 / math.sqrt(HEAD_DIM)
    split_rows = triples.reshape(frames, sites, 3, HEADS, HEAD_DIM)
    scores = (
        jnp.einsum(
            "fshd,gshd->shfg",
            split_rows[:, :, 0],
            split_rows[:, :, 1],
            preferred_element_type=jnp.float32,
        )
        * score_scale
    )
    weights = jax.nn.softmax(scores, axis=-1).astype(jnp.bfloat16)
    attended = jnp.einsum(
        "shfg,gshd->fshd", weights, split_rows[:, :, 2], preferred_element_type=jnp.float32
    )
    return attended.astype(jnp.bfloat16).reshape(frames, sites, triple_width // 3)


def on_device(video, modulation, spatial_input, spatial_output, temporal_input, temporal_output):
    halfway = attend_space(video, modulation, spatial_input, spatial_output)
    count_local, length, features = halfway.shape
    devices = lax.axis_size("wide")
    per_device = length // devices
    normed = normalize(halfway, modulation[3], modulation[4])
    triples = jnp.dot(
        normed.reshape(count_local * length, features),
        temporal_input,
        preferred_element_type=jnp.float32,
    )
    triples = triples.astype(jnp.bfloat16).reshape(count_local, devices, per_device, 3 * features)
    attended = attend_time(
        lax.all_to_all(triples, "wide", split_axis=1, concat_axis=0, tiled=True)[:, 0]
    )[:, None]
    returned = lax.all_to_all(attended, "wide", split_axis=0, concat_axis=1, tiled=True)
    branch = jnp.dot(
        returned.reshape(count_local * length, features),
        temporal_output,
        preferred_element_type=jnp.float32,
    )
    result = halfway.astype(jnp.float32) + modulation[5] * branch.reshape(
        count_local, length, features
    )
    return result.astype(jnp.bfloat16)


def solution(mesh):
    placed = (P(("groups", "wide"), None, None), P("groups", None), P(), P(), P(), P())
    return jax.shard_map(
        on_device,
        mesh=mesh,
        in_specs=placed,
        out_specs=P(("groups", "wide"), None, None),
        check_vma=False,
    )
```

profile of v0, /device:TPU:1, one launch (start us, length us, event | category | flops | bytes accessed | tf_op | source)
XLA Modules:
  0.0 860.9 jit_solution(17176309826605197174)
XLA Ops:
  0.0 3.2 convert_reduce_fusion.1
  3.2 4.5 fusion.20
  8.4 1.9 fusion.23
  10.3 21.3 %convolution_convert_fusion.1 = bf16[2048,3456]{1,0:T(8,128)(2,1)} fusion(bf16[2048,1152]{1,0:T(8,128)(2,1)S(1)} %bitcast.82, bf16[1152,3456]{1,0:T(8,128)(2,1)S(1)} %copy-done.9), kind=kOutput, calls=%fused_computation.12 | convolution fusion | flops 16314531840 | bytes 26836992 | tf_op jit(solution)/shard_map/dot_general | solution.py:26
  31.6 49.4 %reshape.74 = bf16[2,1024,3,16,72]{4,3,2,1,0:T(8,128)(2,1)} reshape(bf16[2048,3456]{1,0:T(8,128)(2,1)} %convolution_convert_fusion.1) | data formatting | bytes 28311552 | tf_op jit(solution)/shard_map/reshape | solution.py:31
  81.0 17.1 %fusion.50 = (bf16[2,1024,1,16,72]{4,3,2,1,0:T(8,128)(2,1)}, bf16[2,1024,1,16,72]{4,3,2,1,0:T(8,128)(2,1)}, bf16[2,1024,1,16,72]{4,3,2,1,0:T(8,128)(2,1)}) fusion(bf16[2,1024,3,16,72]{4,3,2,1,0:T(8,128)(2,1)} %reshape.74), kind=kLoop, calls=%fused_computation.65 | loop fusion | bytes 28311552 | tf_op jit(solution)/shard_map/slice | solution.py:43
  98.1 11.5 %copy.45 = bf16[2,1024,1,16,72]{1,4,3,0,2:T(8,128)(2,1)} copy(bf16[2,1024,1,16,72]{4,3,2,1,0:T(8,128)(2,1)} %get-tuple-element.14) | data formatting | bytes 9437184
  109.6 11.5 %copy.46 = bf16[2,1024,1,16,72]{1,4,3,0,2:T(8,128)(2,1)} copy(bf16[2,1024,1,16,72]{4,3,2,1,0:T(8,128)(2,1)} %get-tuple-element.15) | data formatting | bytes 9437184
  121.1 11.5 %copy.47 = bf16[2,1024,1,16,72]{1,4,3,0,2:T(8,128)(2,1)} copy(bf16[2,1024,1,16,72]{4,3,2,1,0:T(8,128)(2,1)} %get-tuple-element.16) | data formatting | bytes 9437184
  132.6 52.3 %fusion.51 = (f32[2,16,1024]{2,1,0:T(8,128)S(1)}, f32[2,16,1024,1024]{2,3,1,0:T(8,128)}) fusion(bf16[2,1024,1,16,72]{1,4,3,0,2:T(8,128)(2,1)} %copy.47, bf16[2,1024,1,16,72]{1,4,3,0,2:T(8,128)(2,1)} %copy.46), kind=kOutput, calls=%fused_computation.66 | convolution fusion | flops 4932502528 | bytes 143785984 | tf_op jit(solution)/shard_map/sub | solution.py:41
  184.9 44.9 %fusion.42 = bf16[2,16,72,1024]{3,2,1,0:T(8,128)(2,1)} fusion(f32[2,16,1024,1024]{2,3,1,0:T(8,128)} %get-tuple-element.18, f32[2,16,1024]{2,1,0:T(8,128)S(1)} %get-tuple-element.17, bf16[2,1024,1,16,72]{1,4,3,0,2:T(8,128)(2,1)} %copy.45), kind=kOutput, calls=%fused_computation.49 | convolution fusion | flops 4901306368 | bytes 143785984 | tf_op jit(solution)/shard_map/fhqk,fkhd->fqhd/dot_general | solution.py:42
  229.8 22.1 %convert_reduce_fusion = (f32[2,1024]{1,0:T(2,128)S(1)}, bf16[2,1024,1152]{2,1,0:T(8,128)(2,1)S(1)}) fusion(bf16[2,1024,1152]{1,2,0:T(8,128)(2,1)} %bitcast.85, bf16[1152,1152]{1,0:T(8,128)(2,1)S(1)} %copy-done, f32[1152]{0:T(1024)S(1)} %copy-done.8, bf16[2,1024,1152]{2,1,0:T(8,128)(2,1)} %param.6), kind=kOutput, calls=%fused_computation.17 | convolution fusion | flops 5449971712 | bytes 16822784 | tf_op jit(solution)/shard_map/dot_general | solution.py:45
  256.0 22.0 %convolution_convert_fusion = bf16[2048,3456]{1,0:T(8,128)(2,1)S(1)} fusion(bf16[2048,1152]{1,0:T(8,128)(2,1)S(1)} %bitcast.83, bf16[1152,3456]{1,0:T(8,128)(2,1)} %param.10), kind=kOutput, calls=%fused_computation.11 | convolution fusion | flops 16314531840 | bytes 26836992 | tf_op jit(solution)/shard_map/dot_general | solution.py:81
  277.9 3.6 copy.32
  281.5 313.4 %all_to_all.30 = bf16[2,16,64,3456]{3,2,0,1:T(8,128)(2,1)} all-to-all(bf16[2,16,64,3456]{3,2,0,1:T(8,128)(2,1)S(1)} %copy.32), channel_id=1, replica_groups=mesh['groups'=2,'wide'=16] {'wide'}, dimensions={1} | all-to-all | bytes 28311552 | tf_op jit(solution)/shard_map/all_to_all | solution.py:88
  594.9 49.4 %reshape_squeeze.3 = bf16[32,64,3,16,72]{4,3,2,1,0:T(8,128)(2,1)} reshape(bf16[16,2,1,64,3456]{4,3,1,0,2:T(8,128)(2,1)} %bitcast.76) | data formatting | bytes 28311552 | tf_op jit(solution)/shard_map/reshape;squeeze | solution.py:58
  644.3 17.5 %fusion.49 = (bf16[32,64,1,16,72]{4,3,2,1,0:T(8,128)(2,1)}, bf16[32,64,1,16,72]{4,3,2,1,0:T(8,128)(2,1)}, bf16[32,64,1,16,72]{4,3,2,1,0:T(8,128)(2,1)}) fusion(bf16[32,64,3,16,72]{4,3,2,1,0:T(8,128)(2,1)} %reshape_squeeze.3), kind=kLoop, calls=%fused_computation.64 | loop fusion | bytes 28311552 | tf_op jit(solution)/shard_map/slice | solution.py:70
  661.8 22.1 %fusion.27 = f32[64,16,32,32]{2,3,1,0:T(8,128)} fusion(bf16[32,64,1,16,72]{4,3,2,1,0:T(8,128)(2,1)} %get-tuple-element.13, bf16[32,64,1,16,72]{4,3,2,1,0:T(8,128)(2,1)} %get-tuple-element.12), kind=kOutput, calls=%fused_computation.37 | convolution fusion | flops 150994944 | bytes 13631488 | tf_op jit(solution)/shard_map/fshd,gshd->shfg/dot_general | solution.py:60
  683.8 19.3 %fusion.60 = (f32[64,16,32]{2,1,0:T(8,128)S(1)}, f32[64,16,32,32]{2,3,1,0:T(8,128)}) fusion(f32[64,16,32,32]{2,3,1,0:T(8,128)} %fusion.27), kind=kOutput, calls=%fused_computation.67 | output fusion | flops 4194335 | bytes 8519680 | tf_op jit(solution)/shard_map/sub | solution.py:68
  703.1 14.1 %convert_bitcast_fusion = bf16[32,64,16,72]{3,0,2,1:T(8,128)(2,1)} fusion(f32[64,16,32,32]{2,3,1,0:T(8,128)} %get-tuple-element.22, f32[64,16,32]{2,1,0:T(8,128)S(1)} %get-tuple-element.21, bf16[32,64,1,16,72]{4,3,2,1,0:T(8,128)(2,1)} %get-tuple-element.11), kind=kOutput, calls=%fused_computation.40 | convolution fusion | flops 155451392 | bytes 13762560 | tf_op jit(solution)/shard_map/shfg,gshd->fshd/dot_general | solution.py:69
  717.2 9.8 %copy.37 = bf16[32,64,16,72]{3,2,1,0:T(8,128)(2,1)} copy(bf16[32,64,16,72]{3,0,2,1:T(8,128)(2,1)} %convert_bitcast_fusion) | data formatting | bytes 9437184 | tf_op jit(solution)/shard_map/convert_element_type | solution.py:72
  727.1 13.8 %broadcast_in_dim_reshape.3 = bf16[32,1,64,1152]{3,2,0,1:T(8,128)(2,1)} reshape(bf16[32,64,16,72]{3,2,1,0:T(8,128)(2,1)} %copy.37) | data formatting | bytes 9437184 | tf_op jit(solution)/shard_map/broadcast_in_dim;reshape | solution.py:87
  740.8 110.0 %all_to_all.31 = bf16[32,1,64,1152]{3,2,1,0:T(8,128)(2,1)S(1)} all-to-all(bf16[32,1,64,1152]{3,2,1,0:T(8,128)(2,1)} %bitcast.77), channel_id=1, replica_groups=mesh['groups'=2,'wide'=16] {'wide'}, dimensions={0} | all-to-all | bytes 9437184 | tf_op jit(solution)/shard_map/all_to_all | solution.py:90
  851.9 8.6 fusion.25
  (35 shorter events, 5.8 us)
Async XLA Ops:
  0.0 229.8 %copy-start = (bf16[1152,1152]{1,0:T(8,128)(2,1)S(1)}, bf16[1152,1152]{1,0:T(8,128)(2,1)}, u32[]{:S(2)}) copy-start(bf16[1152,1152]{1,0:T(8,128)(2,1)} %param.9) | copy-start | bytes 7962628
  0.0 8.4 copy-start.2
  0.0 7.7 copy-start.6
  0.0 10.3 %copy-start.9 = (bf16[1152,3456]{1,0:T(8,128)(2,1)S(1)}, bf16[1152,3456]{1,0:T(8,128)(2,1)}, u32[]{:S(2)}) copy-start(bf16[1152,3456]{1,0:T(8,128)(2,1)} %param.8) | copy-start | bytes 23887876
  184.9 44.9 %copy-start.8 = (f32[1152]{0:T(1024)S(1)}, f32[1152]{0:T(1024)}, u32[]{:S(2)}) copy-start(f32[1152]{0:T(1024)} %get-tuple-element.8) | copy-start | bytes 13828
  229.8 24.3 %copy-start.4 = (f32[1152]{0:T(1024)S(1)}, f32[1152]{0:T(1024)}, u32[]{:S(2)}) copy-start(f32[1152]{0:T(1024)} %get-tuple-element.9) | copy-start | bytes 13828
  229.8 24.3 %copy-start.5 = (f32[1152]{0:T(1024)S(1)}, f32[1152]{0:T(1024)}, u32[]{:S(2)}) copy-start(f32[1152]{0:T(1024)} %get-tuple-element.10) | copy-start | bytes 13828
  251.9 2.2 copy-start.3
  740.8 110.5 %slice-start = ((s8[4718592]{0:T(1024)(128)(4,1)}), s8[4194304]{0:T(1024)(128)(4,1)S(1)}, s32[]{:S(2)}) async-start(s8[4718592]{0:T(1024)(128)(4,1)} %bitcast.78), calls=%async_computation.2 | async-start | bytes 8388608
  740.8 110.5 %copy-start.7 = (f32[1152]{0:T(1024)S(1)}, f32[1152]{0:T(1024)}, u32[]{:S(2)}) copy-start(f32[1152]{0:T(1024)} %get-tuple-element.5) | copy-start | bytes 13828
  740.8 110.5 %copy-start.10 = (bf16[1152,1152]{1,0:T(8,128)(2,1)S(1)}, bf16[1152,1152]{1,0:T(8,128)(2,1)}, u32[]{:S(2)}) copy-start(bf16[1152,1152]{1,0:T(8,128)(2,1)} %param.11) | copy-start | bytes 7962628
  850.9 1.0 slice-start.1
  851.9 8.6 copy-start.1
where the time goes:
time: 871 us; the launch traced here: 861 us
  blocking collectives  423 us (49%)
  matrix products  207 us (24%)
  local copies, waits for them, and re-layouts  197 us (23%)
  other arithmetic  32.9 us (4%)
    all_to_all x1, blocking collectives, on_device(): lax.all_to_all(triples, 'wide', split_axis=1, concat_axis=0, tiled=True)  313 us
    all_to_all x1, blocking collectives, on_device(): lax.all_to_all(attended, 'wide', split_axis=0, concat_axis=1, tiled=True)  110 us
    sub x1, matrix products, attend_space(): weights = jax.nn.softmax(scores, axis=-1).astype(jnp.bfloat16)  52.3 us
    another operation x1, local copies, waits for them, and re-layouts, attend_time(): split_rows = triples.reshape(frames, sites, 3, HEADS, HEAD_DIM)  49.4 us
    reshape x1, local copies, waits for them, and re-layouts, attend_space(): triples.astype(jnp.bfloat16)  49.4 us
    dot_general x1, matrix products, attend_space(): jnp.einsum('fhqk,fkhd->fqhd', weights, triples[:, :, 2], preferred_elemen...  44.9 us
    unnamed x29, local copies, waits for them, and re-layouts  35.9 us
    dot_general x1, matrix products, attend_space(): jnp.dot(attended.reshape(count_local * length, features), spatial_output,...  22.1 us

commit v1 on v0

--- a/solution.py
+++ b/solution.py
@@ -7,6 +7,13 @@
 HEADS = 16
 HEAD_DIM = 72
 epsilon = 1e-06
+
+
+def stacked_exchange(value, name, split, join):
+    size = lax.axis_size(name)
+    blocks = jnp.stack(jnp.split(value, size, axis=split), axis=0)
+    blocks = lax.all_to_all(blocks, name, split_axis=0, concat_axis=0)
+    return jnp.concatenate(blocks, axis=join)
 
 
 def normalize(stream, offset_row, stretch):
@@ -87,7 +94,7 @@
     attended = attend_time(
         lax.all_to_all(triples, "wide", split_axis=1, concat_axis=0, tiled=True)[:, 0]
     )[:, None]
-    returned = lax.all_to_all(attended, "wide", split_axis=0, concat_axis=1, tiled=True)
+    returned = stacked_exchange(attended, "wide", 0, 1)
     branch = jnp.dot(
         returned.reshape(count_local * length, features),
         temporal_output,

time: 871 us -> 913 us (1.048)
  local copies, waits for them, and re-layouts: 197 us -> 250 us
  matrix products: 207 us -> 196 us
    split x0 -> x17, local copies, waits for them, and re-layouts: none -> 35.8 us  [stacked_exchange(): blocks = jnp.stack(jnp.split(value, size, axis=split), axis=0)]
    another operation x1 -> x17, local copies, waits for them, and re-layouts: 13.8 us -> 29.6 us  [stacked_exchange(): blocks = jnp.stack(jnp.split(value, size, axis=split), axis=0)]
    dot_general x1, matrix products: 22.1 us -> 10.6 us  [attend_space(): jnp.dot(attended.reshape(count_local * length, features), spatial_output,...]
    unnamed x29 -> x50, local copies, waits for them, and re-layouts: 35.9 us -> 46.9 us
    convert_element_type x1 -> x0, local copies, waits for them, and re-layouts: 9.83 us -> none  [attend_time(): attended.astype(jnp.bfloat16).reshape(frames, sites, triple_width // 3)]
where the time goes in v1:
time: 913 us; the launch traced here: 902 us
  blocking collectives  423 us (46%)
  local copies, waits for them, and re-layouts  250 us (27%)
  matrix products  196 us (21%)
  other arithmetic  33 us (4%)
    all_to_all x1, blocking collectives, on_device(): lax.all_to_all(triples, 'wide', split_axis=1, concat_axis=0, tiled=True)  313 us
    all_to_all x1, blocking collectives, stacked_exchange(): blocks = lax.all_to_all(blocks, name, split_axis=0, concat_axis=0)  110 us
    sub x1, matrix products, attend_space(): weights = jax.nn.softmax(scores, axis=-1).astype(jnp.bfloat16)  52.5 us
    another operation x1, local copies, waits for them, and re-layouts, attend_time(): split_rows = triples.reshape(frames, sites, 3, HEADS, HEAD_DIM)  49.4 us
    reshape x1, local copies, waits for them, and re-layouts, attend_space(): triples.astype(jnp.bfloat16)  49.4 us
    unnamed x50, local copies, waits for them, and re-layouts  46.9 us
    dot_general x1, matrix products, attend_space(): jnp.einsum('fhqk,fkhd->fqhd', weights, triples[:, :, 2], preferred_elemen...  44.9 us
    split x17, local copies, waits for them, and re-layouts, stacked_exchange(): blocks = jnp.stack(jnp.split(value, size, axis=split), axis=0)  35.8 us

profile of v1, /device:TPU:1, one launch (start us, length us, event | category | flops | bytes accessed | tf_op | source)
XLA Modules:
  0.0 902.4 jit_solution(11895633505284858421)
XLA Ops:
  0.0 3.2 convert_reduce_fusion.1
  3.2 4.5 fusion.20
  10.3 21.3 %convolution_convert_fusion.1 = bf16[2048,3456]{1,0:T(8,128)(2,1)} fusion(bf16[2048,1152]{1,0:T(8,128)(2,1)S(1)} %bitcast.108, bf16[1152,3456]{1,0:T(8,128)(2,1)S(1)} %copy-done.12), kind=kOutput, calls=%fused_computation.12 | convolution fusion | flops 16314531840 | bytes 26836992 | tf_op jit(solution)/shard_map/dot_general | solution.py:33
  31.6 49.4 %reshape.108 = bf16[2,1024,3,16,72]{4,3,2,1,0:T(8,128)(2,1)} reshape(bf16[2048,3456]{1,0:T(8,128)(2,1)} %convolution_convert_fusion.1) | data formatting | bytes 28311552 | tf_op jit(solution)/shard_map/reshape | solution.py:38
  81.0 17.1 %fusion.50 = (bf16[2,1024,1,16,72]{4,3,2,1,0:T(8,128)(2,1)}, bf16[2,1024,1,16,72]{4,3,2,1,0:T(8,128)(2,1)}, bf16[2,1024,1,16,72]{4,3,2,1,0:T(8,128)(2,1)}) fusion(bf16[2,1024,3,16,72]{4,3,2,1,0:T(8,128)(2,1)} %reshape.108), kind=kLoop, calls=%fused_computation.81 | loop fusion | bytes 28311552 | tf_op jit(solution)/shard_map/slice | solution.py:50
  98.1 11.5 %copy.46 = bf16[2,1024,1,16,72]{1,4,3,0,2:T(8,128)(2,1)} copy(bf16[2,1024,1,16,72]{4,3,2,1,0:T(8,128)(2,1)} %get-tuple-element.14) | data formatting | bytes 9437184
  109.6 11.5 %copy.47 = bf16[2,1024,1,16,72]{1,4,3,0,2:T(8,128)(2,1)} copy(bf16[2,1024,1,16,72]{4,3,2,1,0:T(8,128)(2,1)} %get-tuple-element.15) | data formatting | bytes 9437184
  121.1 11.5 %copy.48 = bf16[2,1024,1,16,72]{1,4,3,0,2:T(8,128)(2,1)} copy(bf16[2,1024,1,16,72]{4,3,2,1,0:T(8,128)(2,1)} %get-tuple-element.16) | data formatting | bytes 9437184
  132.6 52.5 %fusion.52 = (f32[2,16,1024]{2,1,0:T(8,128)S(1)}, f32[2,16,1024,1024]{2,3,1,0:T(8,128)}) fusion(bf16[2,1024,1,16,72]{1,4,3,0,2:T(8,128)(2,1)} %copy.48, bf16[2,1024,1,16,72]{1,4,3,0,2:T(8,128)(2,1)} %copy.47), kind=kOutput, calls=%fused_computation.83 | convolution fusion | flops 4932502528 | bytes 143785984 | tf_op jit(solution)/shard_map/sub | solution.py:48
  185.1 44.9 %fusion.42 = bf16[2,16,72,1024]{3,2,1,0:T(8,128)(2,1)} fusion(f32[2,16,1024,1024]{2,3,1,0:T(8,128)} %get-tuple-element.34, f32[2,16,1024]{2,1,0:T(8,128)S(1)} %get-tuple-element.33, bf16[2,1024,1,16,72]{1,4,3,0,2:T(8,128)(2,1)} %copy.46), kind=kOutput, calls=%fused_computation.49 | convolution fusion | flops 4901306368 | bytes 143785984 | tf_op jit(solution)/shard_map/fhqk,fkhd->fqhd/dot_general | solution.py:49
  230.0 10.6 %convert_reduce_fusion = (f32[2,1024]{1,0:T(2,128)S(1)}, bf16[2,1024,1152]{2,1,0:T(8,128)(2,1)S(1)}) fusion(bf16[2,1024,1152]{1,2,0:T(8,128)(2,1)} %bitcast.111, bf16[1152,1152]{1,0:T(8,128)(2,1)S(1)} %copy-done, f32[1152]{0:T(1024)S(1)} %copy-done.11, bf16[2,1024,1152]{2,1,0:T(8,128)(2,1)} %param.6), kind=kOutput, calls=%fused_computation.17 | convolution fusion | flops 5449971712 | bytes 16822784 | tf_op jit(solution)/shard_map/dot_general | solution.py:52
  244.7 22.0 %convolution_convert_fusion = bf16[2048,3456]{1,0:T(8,128)(2,1)S(1)} fusion(bf16[2048,1152]{1,0:T(8,128)(2,1)S(1)} %bitcast.109, bf16[1152,3456]{1,0:T(8,128)(2,1)} %param.10), kind=kOutput, calls=%fused_computation.11 | convolution fusion | flops 16314531840 | bytes 26836992 | tf_op jit(solution)/shard_map/dot_general | solution.py:88
  266.7 3.6 copy.19
  270.3 313.4 %all_to_all.20 = bf16[2,16,64,3456]{3,2,0,1:T(8,128)(2,1)} all-to-all(bf16[2,16,64,3456]{3,2,0,1:T(8,128)(2,1)S(1)} %copy.19), channel_id=1, replica_groups=mesh['groups'=2,'wide'=16] {'wide'}, dimensions={1} | all-to-all | bytes 28311552 | tf_op jit(solution)/shard_map/all_to_all | solution.py:95
  583.6 49.4 %reshape_squeeze.3 = bf16[32,64,3,16,72]{4,3,2,1,0:T(8,128)(2,1)} reshape(bf16[16,2,1,64,3456]{4,3,1,0,2:T(8,128)(2,1)} %bitcast.103) | data formatting | bytes 28311552 | tf_op jit(solution)/shard_map/reshape;squeeze | solution.py:65
  633.0 17.5 %fusion.49 = (bf16[32,64,1,16,72]{4,3,2,1,0:T(8,128)(2,1)}, bf16[32,64,1,16,72]{4,3,2,1,0:T(8,128)(2,1)}, bf16[32,64,1,16,72]{4,3,2,1,0:T(8,128)(2,1)}) fusion(bf16[32,64,3,16,72]{4,3,2,1,0:T(8,128)(2,1)} %reshape_squeeze.3), kind=kLoop, calls=%fused_computation.80 | loop fusion | bytes 28311552 | tf_op jit(solution)/shard_map/slice | solution.py:77
  650.5 22.1 %fusion.27 = f32[64,16,32,32]{2,3,1,0:T(8,128)} fusion(bf16[32,64,1,16,72]{4,3,2,1,0:T(8,128)(2,1)} %get-tuple-element.13, bf16[32,64,1,16,72]{4,3,2,1,0:T(8,128)(2,1)} %get-tuple-element.12), kind=kOutput, calls=%fused_computation.37 | convolution fusion | flops 150994944 | bytes 13631488 | tf_op jit(solution)/shard_map/fshd,gshd->shfg/dot_general | solution.py:67
  672.6 19.5 %fusion.61 = (f32[64,16,32]{2,1,0:T(8,128)S(1)}, f32[64,16,32,32]{2,3,1,0:T(8,128)}) fusion(f32[64,16,32,32]{2,3,1,0:T(8,128)} %fusion.27), kind=kOutput, calls=%fused_computation.84 | output fusion | flops 4194335 | bytes 8519680 | tf_op jit(solution)/shard_map/sub | solution.py:75
  692.1 14.1 %convert_bitcast_fusion = bf16[32,64,16,72]{3,0,2,1:T(8,128)(2,1)} fusion(f32[64,16,32,32]{2,3,1,0:T(8,128)} %get-tuple-element.38, f32[64,16,32]{2,1,0:T(8,128)S(1)} %get-tuple-element.37, bf16[32,64,1,16,72]{4,3,2,1,0:T(8,128)(2,1)} %get-tuple-element.11), kind=kOutput, calls=%fused_computation.40 | convolution fusion | flops 155451392 | bytes 13762560 | tf_op jit(solution)/shard_map/shfg,gshd->fshd/dot_general | solution.py:76
  706.2 16.7 %fusion.51 = (bf16[2,64,16,72]{3,0,2,1:T(2,128)(2,1)S(1)}, bf16[2,64,16,72]{3,0,2,1:T(2,128)(2,1)}, bf16[2,64,16,72]{3,0,2,1:T(2,128)(2,1)}, bf16[2,64,16,72]{3,...) fusion(bf16[32,64,16,72]{3,0,2,1:T(8,128)(2,1)} %convert_bitcas, ...), kind=kLoop, calls=%fused_computation.82 | loop fusion | bytes 9437184 | tf_op jit(solution)/shard_map/split | solution.py:14
  747.9 2.3 stack.60
  760.4 2.3 stack.57
  782.8 109.8 %all_to_all.21 = bf16[16,2,1,64,1152]{4,3,1,2,0:T(8,128)(2,1)S(1)} all-to-all(bf16[16,2,1,64,1152]{4,3,1,2,0:T(8,128)(2,1)S(1)} %constant_dynamic-update-slice_fusion), channel_id=1, replica_groups=mesh['groups'=2,'wide'=16] {'wide'}, dimensions={0} | all-to-all | bytes 9437184 | tf_op jit(solution)/shard_map/all_to_all | solution.py:15
  893.6 8.6 fusion.25
  (88 shorter events, 62.9 us)
Async XLA Ops:
  0.0 230.0 %copy-start = (bf16[1152,1152]{1,0:T(8,128)(2,1)S(1)}, bf16[1152,1152]{1,0:T(8,128)(2,1)}, u32[]{:S(2)}) copy-start(bf16[1152,1152]{1,0:T(8,128)(2,1)} %param.9) | copy-start | bytes 7962628
  0.0 8.4 copy-start.2
  0.0 7.7 copy-start.9
  0.0 10.3 %copy-start.12 = (bf16[1152,3456]{1,0:T(8,128)(2,1)S(1)}, bf16[1152,3456]{1,0:T(8,128)(2,1)}, u32[]{:S(2)}) copy-start(bf16[1152,3456]{1,0:T(8,128)(2,1)} %param.8) | copy-start | bytes 23887876
  185.1 44.9 %copy-start.11 = (f32[1152]{0:T(1024)S(1)}, f32[1152]{0:T(1024)}, u32[]{:S(2)}) copy-start(f32[1152]{0:T(1024)} %get-tuple-element.8) | copy-start | bytes 13828
  230.0 12.8 %copy-start.7 = (f32[1152]{0:T(1024)S(1)}, f32[1152]{0:T(1024)}, u32[]{:S(2)}) copy-start(f32[1152]{0:T(1024)} %get-tuple-element.9) | copy-start | bytes 13828
  230.0 12.8 %copy-start.8 = (f32[1152]{0:T(1024)S(1)}, f32[1152]{0:T(1024)}, u32[]{:S(2)}) copy-start(f32[1152]{0:T(1024)} %get-tuple-element.10) | copy-start | bytes 13828
  240.6 2.2 copy-start.3
  767.1 15.6 %copy-start.4 = (bf16[1,2,1,64,1152]{4,3,1,2,0:T(8,128)(2,1)S(1)}, bf16[1,2,1,64,1152]{4,3,1,2,0:T(8,128)(2,1)}, u32[]{:S(2)}) copy-start(bf16[1,2,1,64,1152]{4,3,1,2,0:T(8,128)(2,1)} %stack.65) | copy-start | bytes 884740
  768.4 10.2 %copy-start.5 = (bf16[1,2,1,64,1152]{4,3,1,2,0:T(8,128)(2,1)S(1)}, bf16[1,2,1,64,1152]{4,3,1,2,0:T(8,128)(2,1)}, u32[]{:S(2)}) copy-start(bf16[1,2,1,64,1152]{4,3,1,2,0:T(8,128)(2,1)} %stack.60) | copy-start | bytes 884740
  769.7 8.9 copy-start.6
  782.7 110.3 %slice-start = ((s8[4718592]{0:T(1024)(128)(4,1)}), s8[4194304]{0:T(1024)(128)(4,1)S(1)}, s32[]{:S(2)}) async-start(s8[4718592]{0:T(1024)(128)(4,1)} %bitcast.104), calls=%async_computation.2 | async-start | bytes 8388608
  782.8 110.3 %copy-start.10 = (f32[1152]{0:T(1024)S(1)}, f32[1152]{0:T(1024)}, u32[]{:S(2)}) copy-start(f32[1152]{0:T(1024)} %get-tuple-element.5) | copy-start | bytes 13828
  782.8 110.3 %copy-start.13 = (bf16[1152,1152]{1,0:T(8,128)(2,1)S(1)}, bf16[1152,1152]{1,0:T(8,128)(2,1)}, u32[]{:S(2)}) copy-start(bf16[1152,1152]{1,0:T(8,128)(2,1)} %param.11) | copy-start | bytes 7962628
  892.6 1.0 slice-start.1
  893.6 8.6 copy-start.1
